TPU v7x, 32 devices: a whole 2x2x4 slice. The times are simulated.
32 devices in a mesh: front: 4 (over z), row: 4 (over x, core), col: 2 (over y).
Axes of the slice: x: 2, y: 2, z: 4, core: 2. Of those that a mesh axis runs over, the one named last changes fastest.
Arguments:
- own_rows: float32 [4, 1536, 4096], P('front', 'row', 'col'), may hold values from -1.5 to 1.5
- child_rows: float32 [8192, 4096], P(('front', 'row'), 'col'), may hold values from -3 to 3
- child_dest: int32 [8192, 1], P(('front', 'row')), may hold values from 0 to 3; in each aligned block of 512 rows (0 to 511, 512 to 1023, ...) at most 256 rows name the same one
- child_stair: int32 [8192], P(('front', 'row')), may hold values from 0 to 7
Outputs:
- r_factor: float32 [4, 1024, 4096], P('front', 'row', 'col')
Inputs may be any that keep to these rules, and one draw needn't show every extreme that they name: `child_dest`: among the 512 rows of one device at most 256 name one parent, and in every draw some device has exactly 256 rows for some parent.
All inputs are finite; a program needn't handle non-finite values.
Results may differ from a plain program's by a relative error of at most 0.0003.
Values sent between devices are 32-bit elements; how exact they have to be, the bound alone decides.
A program may use at most 128 MiB of HBM per device.

v0:
```python
import jax
import jax.numpy as jnp
from jax import lax
from jax.sharding import PartitionSpec as P

PANEL_COLUMNS = 512
PANEL_COUNT = 2
STAIR_BLK = 128


def panel_factor(sums_block, panel_cols):
    lower_cholesky_factor = jnp.linalg.cholesky(sums_block[1])
    factor_rows = jax.scipy.linalg.solve_triangular(
        lower_cholesky_factor, sums_block[0], lower=True
    )
    basis = jax.scipy.linalg.solve_triangular(lower_cholesky_factor, panel_cols.T, lower=True).T
    return (factor_rows, basis)


def body(own_rows, child_rows, child_dest, child_stair):
    n_front = lax.axis_size("front")
    row_count = lax.axis_size("row")
    n_col = lax.axis_size("col")
    source_rows = child_rows.shape[0]
    half_cols = child_rows.shape[1]
    capacity = max(2, 2 * source_rows // n_front)
    col_index = lax.axis_index("col")
    global_cols = col_index * half_cols + lax.broadcasted_iota(
        jnp.int32, (source_rows, half_cols), 1
    )
    masked_rows = jnp.where(global_cols >= (child_stair * STAIR_BLK)[:, None], child_rows, 0.0)
    targets = child_dest[:, 0]
    onehot = (targets[:, None] == jnp.arange(n_front, dtype=jnp.int32)[None, :]).astype(jnp.int32)
    slot = jnp.sum((jnp.cumsum(onehot, axis=0) - onehot) * onehot, axis=1)
    eliminated_panel = PANEL_COUNT * PANEL_COLUMNS
    quarter_block = eliminated_panel // row_count
    row_start = lax.axis_index("row") * quarter_block
    sub_cap = capacity // n_col
    position = targets * capacity + slot % n_col * sub_cap + slot // n_col
    send_block = (
        jnp.zeros((n_front * capacity, half_cols), jnp.float32).at[position].set(masked_rows)
    )
    received = lax.all_to_all(send_block, ("front", "col"), split_axis=0, concat_axis=0, tiled=True)
    received = (
        received.reshape(n_front, n_col, sub_cap, half_cols)
        .transpose(0, 2, 1, 3)
        .reshape(n_front * sub_cap, n_col * half_cols)
    )
    own_whole = lax.all_to_all(own_rows[0], "col", split_axis=0, concat_axis=1, tiled=True)
    remaining = jnp.concatenate([own_whole, received], 0)
    blocks = []
    for step in range(PANEL_COUNT):
        start_col = step * PANEL_COLUMNS
        panel_cols = remaining[:, :PANEL_COLUMNS]
        products = jnp.dot(
            panel_cols.T,
            remaining,
            precision=lax.Precision.HIGHEST,
            preferred_element_type=jnp.float32,
        )
        products = lax.psum(products, ("row", "col"))
        factor_rows, basis = panel_factor((products, products[:, :PANEL_COLUMNS]), panel_cols)
        trailing = remaining[:, PANEL_COLUMNS:] - jnp.dot(
            basis,
            factor_rows[:, PANEL_COLUMNS:],
            precision=lax.Precision.HIGHEST,
            preferred_element_type=jnp.float32,
        )
        blocks.append(
            jnp.concatenate([jnp.zeros((PANEL_COLUMNS, start_col), jnp.float32), factor_rows], 1)
        )
        remaining = trailing
    factor_all = jnp.concatenate(blocks, 0)
    mine = lax.dynamic_slice_in_dim(factor_all, row_start, quarter_block, 0)
    mine = lax.dynamic_slice_in_dim(mine, col_index * half_cols, half_cols, 1)
    return mine[None]


def solution(mesh):
    placed = (
        P("front", "row", "col"),
        P(("front", "row"), "col"),
        P(("front", "row"), None),
        P(("front", "row")),
    )
    return jax.shard_map(
        body, mesh=mesh, in_specs=placed, out_specs=P("front", "row", "col"), check_vma=False
    )
```

profile of v0, /device:TPU:0, one launch (start us, length us, event | category | flops | bytes accessed | tf_op | source)
XLA Modules:
  0.0 944.8 jit_solution(17237512085948040899)
XLA Ops:
  6.5 4.4 all-to-all-start
  12.7 9.0 scatter_custom_fusion
  21.7 26.5 %all-to-all-done = f32[2,192,2048]{2,1,0:T(8,128)S(1)} async-done(((f32[2,192,2048]{2,1,0:T(8,128)}), f32[2,192,2048]{2,1,0:T(8,128)S(1)}, u32[]{:S(2)}, u32[]{:S(2)}) %all-to-all-start) | async-done | bytes 3145760 | tf_op jit(solution)/shard_map/all_to_all | solution.py:49
  48.2 5.1 all-to-all-start.1
  54.0 1.9 constant_dynamic-update-slice_fusion.1
  55.9 180.0 %all-to-all-done.1 = f32[8,128,2048]{2,1,0:T(8,128)} async-done(((f32[8,128,2048]{2,1,0:T(8,128)}), f32[8,128,2048]{2,1,0:T(8,128)}, u32[]{:S(2)}, u32[]{:S(2)}) %all-to-all-start.1) | async-done | bytes 8388640 | tf_op jit(solution)/shard_map/all_to_all | solution.py:43
  235.9 15.6 %copy.17 = f32[4,128,2,2048]{3,2,1,0:T(2,128)} copy(f32[4,128,2,2048]{3,1,2,0:T(8,128)} %bitcast.9) | data formatting | bytes 16777216 | tf_op jit(solution)/shard_map/transpose | solution.py:46
  251.5 11.6 %copy.38 = f32[64,8,2,2048]{3,1,2,0:T(8,128)S(1)} copy(f32[64,8,2,2048]{3,2,1,0:T(2,128)} %bitcast.156) | data formatting | bytes 16777216
  264.2 4.3 copy-done
  268.5 23.5 %fusion.47 = f32[512,4096]{0,1:T(8,128)} fusion(f32[704,4096]{1,0:T(8,128)S(1)} %constant_dynamic-update-slice_fusion), kind=kOutput, calls=%fused_computation.62 | convolution fusion | flops 17716740096 | bytes 21364736 | tf_op jit(solution)/shard_map/dot_general | solution.py:55
  292.4 2.6 slice_bitcast_fusion
  294.9 122.5 %all-reduce.5.cloned.1.call-done = f32[512,4096]{0,1:T(8,128)} async-done(((f32[512,4096]{0,1:T(8,128)}), f32[512,4096]{0,1:T(8,128)}) %all-reduce.5.cloned.1.call-update) | async-done | bytes 8388624 | tf_op jit(solution)/shard_map/psum | solution.py:61
  419.0 1.4 fusion.55
  420.5 11.7 %cholesky.286 = f32[128,128]{1,0:T(8,128)S(1)} custom-call(f32[128,128]{1,0:T(8,128)S(1)} %cholesky.426), custom_call_target="Cholesky" | custom-call | tf_op jit(solution)/shard_map/jit(cholesky)/cholesky | solution.py:12
  432.3 9.8 %custom-call.36 = f32[1,128,128]{1,2,0:T(8,128)S(1)} custom-call(f32[1,128,128]{2,1,0:T(8,128)S(1)} %get-tuple-element.61), custom_call_target="InvertDiagBlocksLowerTriangular" | custom-call | tf_op jit(solution)/shard_map/jit(cholesky)/cholesky | solution.py:12
  442.8 11.7 %cholesky.305 = f32[128,128]{1,0:T(8,128)S(1)} custom-call(f32[128,128]{1,0:T(8,128)S(1)} %cholesky.430), custom_call_target="Cholesky" | custom-call | tf_op jit(solution)/shard_map/jit(cholesky)/cholesky | solution.py:12
  454.6 10.2 %custom-call.37 = f32[1,128,128]{1,2,0:T(8,128)S(1)} custom-call(f32[1,128,128]{2,1,0:T(8,128)S(1)} %get-tuple-element.58), custom_call_target="InvertDiagBlocksLowerTriangular" | custom-call | tf_op jit(solution)/shard_map/jit(cholesky)/cholesky | solution.py:12
  465.5 11.7 %cholesky.326 = f32[128,128]{1,0:T(8,128)S(1)} custom-call(f32[128,128]{1,0:T(8,128)S(1)} %cholesky.435), custom_call_target="Cholesky" | custom-call | tf_op jit(solution)/shard_map/jit(cholesky)/cholesky | solution.py:12
  477.2 9.8 %custom-call.38 = f32[1,128,128]{1,2,0:T(8,128)S(1)} custom-call(f32[1,128,128]{2,1,0:T(8,128)S(1)} %get-tuple-element.55), custom_call_target="InvertDiagBlocksLowerTriangular" | custom-call | tf_op jit(solution)/shard_map/jit(cholesky)/cholesky | solution.py:12
  487.6 11.7 %cholesky.343 = f32[128,128]{1,0:T(8,128)S(1)} custom-call(f32[128,128]{1,0:T(8,128)S(1)} %convolution_subtract_fusion.12), custom_call_target="Cholesky" | custom-call | tf_op jit(solution)/shard_map/jit(cholesky)/cholesky | solution.py:12
  504.2 8.0 while.2
  504.9 1.3 bitcast_dynamic-update-slice_fusion.4
  506.9 1.3 bitcast_dynamic-update-slice_fusion.4
  508.9 1.3 bitcast_dynamic-update-slice_fusion.4
  510.9 1.3 bitcast_dynamic-update-slice_fusion.4
  513.3 39.3 %custom-call.31 = f32[4,128,128]{1,2,0:T(8,128)S(1)} custom-call(f32[4,128,128]{2,1,0:T(8,128)S(1)} %get-tuple-element.13), custom_call_target="InvertDiagBlocksLowerTriangular" | custom-call | tf_op jit(solution)/shard_map/jit(_solve_triangular)/triangular_solve | solution.py:13
  552.6 1.5 fusion.59
  554.1 1.5 convolution_subtract_fusion.4
  559.6 3.7 constant_dynamic-update-slice_fusion.5
  563.3 5.9 convolution_subtract_fusion.3
  569.2 2.0 constant_dynamic-update-slice_fusion.4
  571.2 7.4 convolution_subtract_fusion.2
  578.6 2.0 constant_dynamic-update-slice_fusion.3
  580.6 11.0 %fusion.18 = f32[128,4096]{0,1:T(8,128)S(1)} fusion(f32[128,4096]{1,0:T(8,128)S(1)} %get-tuple-element.69, f32[128,4096]{1,0:T(8,128)S(1)} %get-tuple-element.67, f32[128,4096]{1,0:T(8,128)S(1)} %get-tuple-element.65, f32[512,4096]{0,1:T(8,128)S(1)} %bitcast.158, f32[512,512]{1,0:T(8,128)S(1)} %copy-done.6), kind=kOutput, calls=%fused_computation.33 | convolution fusion | flops 2419589120 | bytes 10682368 | tf_op jit(solution)/shard_map/jit(_solve_triangular)/triangular_solve | solution.py:13
  591.5 3.3 constant_dynamic-update-slice_fusion.2
  594.8 5.7 copy-done.7
  600.5 21.4 %slice_subtract_fusion = f32[704,3584]{1,0:T(8,128)S(1)} fusion(f32[704,4096]{1,0:T(8,128)} %copy-done, f32[128,4096]{1,0:T(8,128)} %get-tuple-element.71, f32[128,4096]{1,0:T(8,128)} %copy-done.3, f32[128,4096]{1,0:T(8,128)} %copy-done.2, f32[128,4096]{1,0:T(8,128)} %copy-done.1, f32[128,704]{0,1:T(8,128)} %fusion.97, f32[128,704]{0,1:T(8,128)S(1)} %fusion.95, ...), kind=kOutput, calls=%fused_computation.5 | convolution fusion | flops 15511257088 | bytes 30015488 | tf_op jit(solution)/shard_map/dot_general | solution.py:63
  621.9 21.3 %fusion.38 = f32[512,3584]{0,1:T(8,128)} fusion(f32[704,3584]{1,0:T(8,128)S(1)} %slice_subtract_fusion), kind=kOutput, calls=%fused_computation.52 | convolution fusion | flops 15502147584 | bytes 18874368 | tf_op jit(solution)/shard_map/dot_general | solution.py:55
  643.2 115.7 %all-reduce.7.cloned.1.call-done = f32[512,3584]{0,1:T(8,128)} async-done(((f32[512,3584]{0,1:T(8,128)}), f32[512,3584]{0,1:T(8,128)}) %all-reduce.7.cloned.1.call-update) | async-done | bytes 7340048 | tf_op jit(solution)/shard_map/psum | solution.py:61
  758.9 1.2 slice-done.8
  760.5 1.4 fusion.54
  762.0 11.7 %cholesky.358 = f32[128,128]{1,0:T(8,128)S(1)} custom-call(f32[128,128]{1,0:T(8,128)S(1)} %cholesky.439), custom_call_target="Cholesky" | custom-call | tf_op jit(solution)/shard_map/jit(cholesky)/cholesky | solution.py:12
  773.9 9.8 %custom-call.39 = f32[1,128,128]{1,2,0:T(8,128)S(1)} custom-call(f32[1,128,128]{2,1,0:T(8,128)S(1)} %get-tuple-element.51), custom_call_target="InvertDiagBlocksLowerTriangular" | custom-call | tf_op jit(solution)/shard_map/jit(cholesky)/cholesky | solution.py:12
  784.3 11.7 %cholesky.377 = f32[128,128]{1,0:T(8,128)S(1)} custom-call(f32[128,128]{1,0:T(8,128)S(1)} %cholesky.443), custom_call_target="Cholesky" | custom-call | tf_op jit(solution)/shard_map/jit(cholesky)/cholesky | solution.py:12
  796.1 10.0 %custom-call.40 = f32[1,128,128]{1,2,0:T(8,128)S(1)} custom-call(f32[1,128,128]{2,1,0:T(8,128)S(1)} %get-tuple-element.48), custom_call_target="InvertDiagBlocksLowerTriangular" | custom-call | tf_op jit(solution)/shard_map/jit(cholesky)/cholesky | solution.py:12
  806.7 11.7 %cholesky.398 = f32[128,128]{1,0:T(8,128)S(1)} custom-call(f32[128,128]{1,0:T(8,128)S(1)} %cholesky.448), custom_call_target="Cholesky" | custom-call | tf_op jit(solution)/shard_map/jit(cholesky)/cholesky | solution.py:12
  818.5 9.8 %custom-call.41 = f32[1,128,128]{1,2,0:T(8,128)S(1)} custom-call(f32[1,128,128]{2,1,0:T(8,128)S(1)} %get-tuple-element.45), custom_call_target="InvertDiagBlocksLowerTriangular" | custom-call | tf_op jit(solution)/shard_map/jit(cholesky)/cholesky | solution.py:12
  828.9 11.7 %cholesky.415 = f32[128,128]{1,0:T(8,128)S(1)} custom-call(f32[128,128]{1,0:T(8,128)S(1)} %convolution_subtract_fusion.11), custom_call_target="Cholesky" | custom-call | tf_op jit(solution)/shard_map/jit(cholesky)/cholesky | solution.py:12
  845.9 1.5 select_select_fusion
  847.4 12.0 %while.3 = (s32[]{:T(128)}, f32[512,512]{1,0:T(8,128)}, s32[4,2]{0,1:T(2,128)S(1)}, f32[4,128,128]{2,1,0:T(8,128)S(1)}, s32[]{:T(128)}) while((s32[]{:T(128)}, f32[512,512]{1,0:T(8,128)}, s32[4,2]{0,1:T(2,128)S(1)}, f32[4,128,128]{2,1,0:T(8,128)S(1)}, s32[]{:T(128)}) %tuple.63), condition=%wide.while_cond.1, body=%wide.while_body.1.sunk | while | flops 2 | bytes 131189 | solution.py:13
  848.1 2.5 bitcast_dynamic-update-slice_fusion.5
  851.3 2.3 bitcast_dynamic-update-slice_fusion.5
  854.3 2.3 bitcast_dynamic-update-slice_fusion.5
  857.2 2.2 bitcast_dynamic-update-slice_fusion.5
  860.2 40.1 %custom-call.32 = f32[4,128,128]{1,2,0:T(8,128)S(1)} custom-call(f32[4,128,128]{2,1,0:T(8,128)} %copy-done.8), custom_call_target="InvertDiagBlocksLowerTriangular" | custom-call | tf_op jit(solution)/shard_map/jit(_solve_triangular)/triangular_solve | solution.py:13
  900.3 3.2 fusion.36
  903.5 4.7 convolution_subtract_fusion.1
  908.2 1.7 fusion.82
  910.0 7.0 convolution_subtract_fusion
  916.9 1.7 fusion.80
  918.7 9.7 %fusion.15 = f32[128,3584]{0,1:T(8,128)S(1)} fusion(f32[128,3584]{1,0:T(8,128)S(1)} %fusion.80, f32[128,3584]{1,0:T(8,128)S(1)} %fusion.82, f32[128,3584]{1,0:T(8,128)S(1)} %fusion.36, f32[512,3584]{0,1:T(8,128)S(1)} %bitcast.162, f32[512,512]{1,0:T(8,128)} %get-tuple-element.178), kind=kOutput, calls=%fused_computation.32 | convolution fusion | flops 2117140480 | bytes 9371648 | tf_op jit(solution)/shard_map/jit(_solve_triangular)/triangular_solve | solution.py:13
  928.4 1.7 fusion.79
  930.2 4.0 fusion
  934.2 3.6 dynamic-slice_bitcast_fusion
  (118 shorter events, 26.0 us)
Async XLA Ops:
  6.5 4.4 copy-start.9
  6.5 6.1 copy-start.10
  6.5 41.7 %all-to-all-start = ((f32[2,192,2048]{2,1,0:T(8,128)}), f32[2,192,2048]{2,1,0:T(8,128)S(1)}, u32[]{:S(2)}, u32[]{:S(2)}) async-start(f32[2,192,2048]{2,1,0:T(8,128)} %bitcast.163), calls=%async_computation | async-start | bytes 6291456 | tf_op jit(solution)/shard_map/all_to_all | solution.py:49
  48.2 187.7 %all-to-all-start.1 = ((f32[8,128,2048]{2,1,0:T(8,128)}), f32[8,128,2048]{2,1,0:T(8,128)}, u32[]{:S(2)}, u32[]{:S(2)}) async-start(f32[8,128,2048]{2,1,0:T(8,128)} %bitcast.154), calls=%async_computation.1 | async-start | bytes 16777216 | tf_op jit(solution)/shard_map/all_to_all | solution.py:43
  53.3 364.1 %all-reduce.5.cloned.1.call-start = ((), (), s32[]{:S(2)}) async-start(), calls=%async_computation.2 | async-start | bytes 16777216 | tf_op jit(solution)/shard_map/psum | solution.py:61
  235.9 27.2 %slice-start = ((s8[11534336]{0:T(1024)(128)(4,1)}), s8[4194304]{0:T(1024)(128)(4,1)S(1)}, s32[]{:S(2)}) async-start(s8[11534336]{0:T(1024)(128)(4,1)} %bitcast.152), calls=%async_computation.4 | async-start | bytes 8388608
  235.9 27.2 %slice-start.1 = ((s8[11534336]{0:T(1024)(128)(4,1)}), s8[4194304]{0:T(1024)(128)(4,1)S(1)}, s32[]{:S(2)}) async-start(s8[11534336]{0:T(1024)(128)(4,1)} %bitcast.152), calls=%async_computation.5 | async-start | bytes 8388608
  251.5 11.7 %slice-start.2 = ((s8[11534336]{0:T(1024)(128)(4,1)}), s8[3145728]{0:T(1024)(128)(4,1)S(1)}, s32[]{:S(2)}) async-start(s8[11534336]{0:T(1024)(128)(4,1)} %bitcast.152), calls=%async_computation.6 | async-start | bytes 6291456
  264.2 4.4 copy-start
  292.1 466.9 %all-reduce.7.cloned.1.call-start = ((), (), s32[]{:S(2)}) async-start(), calls=%async_computation.3 | async-start | bytes 14680064 | tf_op jit(solution)/shard_map/psum | solution.py:61
  417.4 1.2 slice-start.5
  504.1 51.9 %copy-start.4 = (f32[512,704]{0,1:T(8,128)S(1)}, f32[512,704]{0,1:T(8,128)}, u32[]{:S(2)}) copy-start(f32[512,704]{0,1:T(8,128)} %slice_bitcast_fusion) | copy-start | bytes 4325380
  512.2 1.1 copy-start.5
  552.6 3.5 copy-start.6
  559.5 11.6 %slice-start.3 = ((s8[8388608]{0:T(1024)(128)(4,1)}), s8[4194304]{0:T(1024)(128)(4,1)S(1)}, s32[]{:S(2)}) async-start(s8[8388608]{0:T(1024)(128)(4,1)} %bitcast.157), calls=%async_computation.7 | async-start | bytes 8388608
  563.3 17.3 %copy-start.1 = (f32[128,4096]{1,0:T(8,128)}, f32[128,4096]{1,0:T(8,128)S(1)}, u32[]{:S(2)}) copy-start(f32[128,4096]{1,0:T(8,128)S(1)} %get-tuple-element.65) | copy-start | bytes 6291460
  563.3 7.9 slice-start.4
  571.1 9.4 copy-start.2
  580.5 11.0 %copy-start.3 = (f32[128,4096]{1,0:T(8,128)}, f32[128,4096]{1,0:T(8,128)S(1)}, u32[]{:S(2)}) copy-start(f32[128,4096]{1,0:T(8,128)S(1)} %get-tuple-element.69) | copy-start | bytes 6291460
  594.8 5.7 copy-start.7
  758.9 1.2 slice-start.8
  847.4 62.5 %slice-start.6 = ((s8[7340032]{0:T(1024)(128)(4,1)}), s8[3145728]{0:T(1024)(128)(4,1)S(1)}, s32[]{:S(2)}) async-start(s8[7340032]{0:T(1024)(128)(4,1)} %bitcast.161), calls=%async_computation.10 | async-start | bytes 6291456
  859.4 0.7 copy-start.8
  903.5 6.5 slice-start.7
Sparse Core Ops, SparseCore 0:
  292.2 125.1 all-reduce.4
  643.3 115.5 all-reduce.6
where the time goes:
time: 950 us; the launch traced here: 945 us
  waiting for transfers between devices  445 us (47%)
  other arithmetic  257 us (27%)
  matrix products  142 us (15%)
  local copies, waits for them, and re-layouts  71.8 us (8%)
  between operations  19.3 us (2%)
  starting transfers between devices  10.3 us (1%)
    psum x2, waiting for transfers between devices, body(): products = lax.psum(products, ('row', 'col'))  238 us
    all_to_all x1, waiting for transfers between devices, body(): lax.all_to_all(send_block, ('front', 'col'), split_axis=0, concat_axis=0,...  180 us
    another operation x29, other arithmetic, panel_factor(): lower_cholesky_factor = jnp.linalg.cholesky(sums_block[1])  158 us
    another operation x5, other arithmetic, panel_factor(): jax.scipy.linalg.solve_triangular(lower_cholesky_factor, sums_block[0], l...  81 us
    another operation x14, matrix products, panel_factor(): jax.scipy.linalg.solve_triangular(lower_cholesky_factor, sums_block[0], l...  64.9 us
    dot_general x2, matrix products, body(): jnp.dot(panel_cols.T, remaining, precision=lax.Precision.HIGHEST, preferr...  44.8 us
    all_to_all x1, waiting for transfers between devices, body(): lax.all_to_all(own_rows[0], 'col', split_axis=0, concat_axis=1, tiled=True)  26.5 us
    unnamed x40, local copies, waits for them, and re-layouts  25.4 us
  transfers between devices with their start and end apart: 4, of which 4 were waited for; matrix products, arithmetic and copies ran while one was open for 2% of the time, Pallas kernels for 0%

commit v1 on v0

v1 whole, which is shorter than its diff:
```python
import functools

import jax
import jax.numpy as jnp
from jax import lax
from jax.experimental import pallas as pl
from jax.experimental.pallas import tpu as pltpu
from jax.sharding import PartitionSpec as P

PANEL_COLUMNS = 512
PANEL_COUNT = 2
STAIR_BLK = 128
BLOCK = 128
HALF = 64
HI = lax.Precision.HIGHEST
TN = (((0,), (0,)), ((), ()))
NT = (((1,), (1,)), ((), ()))


def mm(a, b, dims=(((1,), (0,)), ((), ()))):
    return lax.dot_general(a, b, dims, precision=HI, preferred_element_type=jnp.float32)


def split(x):
    hi = x.astype(jnp.bfloat16)
    return hi, (x - hi.astype(jnp.float32)).astype(jnp.bfloat16)


def gram_kernel(own_lhs, child_lhs, own_rhs, child_rhs, out, lhs_hi, lhs_lo):
    n_own = own_lhs.shape[1]

    @pl.when(pl.program_id(0) == 0)
    def _():
        for src, start in ((own_lhs, 0), (child_lhs, n_own)):
            rows = src.shape[1]
            hi, lo = split(src[0])
            lhs_hi[start : start + rows] = hi
            lhs_lo[start : start + rows] = lo

    own_hi, own_lo = split(own_rhs[0])
    child_hi, child_lo = split(child_rhs[0])
    rhs_hi = jnp.concatenate([own_hi, child_hi], 0)
    rhs_lo = jnp.concatenate([own_lo, child_lo], 0)

    def dot(a, b):
        return lax.dot_general(a, b, TN, preferred_element_type=jnp.float32)

    width = 256
    for start in range(0, out.shape[1], width):
        cols = slice(start, start + width)
        a_hi, a_lo = lhs_hi[:, cols], lhs_lo[:, cols]
        out[0, cols, :] = dot(a_lo, rhs_hi) + dot(a_hi, rhs_lo) + dot(a_hi, rhs_hi)


def gram(own, child, eliminated, parts):
    n_col, own_rows, half_cols = own.shape
    child_rows = child.shape[1]
    per = parts // n_col
    width = half_cols // per
    return pl.pallas_call(
        gram_kernel,
        out_shape=jax.ShapeDtypeStruct((parts, eliminated, width), jnp.float32),
        grid=(parts,),
        in_specs=[
            pl.BlockSpec((1, own_rows, eliminated), lambda q: (0, 0, 0)),
            pl.BlockSpec((1, child_rows, eliminated), lambda q: (0, 0, 0)),
            pl.BlockSpec((1, own_rows, width), lambda q: (q // per, 0, q % per)),
            pl.BlockSpec((1, child_rows, width), lambda q: (q // per, 0, q % per)),
        ],
        out_specs=pl.BlockSpec((1, eliminated, width), lambda q: (q, 0, 0)),
        scratch_shapes=[pltpu.VMEM((own_rows + child_rows, eliminated), jnp.bfloat16)] * 2,
        cost_estimate=pl.CostEstimate(
            flops=6 * (own_rows + child_rows) * eliminated * half_cols * n_col,
            bytes_accessed=4 * (own_rows + child_rows + eliminated) * half_cols * n_col,
            transcendentals=0,
        ),
    )(own, child, own, child)


def small_inverse(block):
    lanes = lax.broadcasted_iota(jnp.int32, (HALF, 2 * HALF), 1)
    rows = lax.broadcasted_iota(jnp.int32, (HALF, 2 * HALF), 0)
    eye = (lanes[:, :HALF] == rows[:, :HALF]).astype(jnp.float32)
    both = jnp.concatenate([block, eye], 1)

    def step(j, m):
        pivot_row = jnp.sum(jnp.where(rows == j, m, 0.0), axis=0, keepdims=True)
        column = jnp.sum(jnp.where(lanes == j, m, 0.0), axis=1, keepdims=True)
        pivot = jnp.sum(jnp.where(lanes[:1] == j, pivot_row, 0.0), axis=1, keepdims=True)
        scale = lax.rsqrt(pivot)
        scaled = pivot_row * scale
        factor = column * scale
        return jnp.where(rows > j, m - factor * scaled, jnp.where(rows == j, scaled, m))

    return lax.fori_loop(0, HALF, step, both)[:, HALF:]


def inverse_kernel(blocks, out, work):
    n = out.shape[0]
    width = blocks.shape[2]
    count = n // BLOCK
    for part in range(blocks.shape[0]):
        work[:, part * width : (part + 1) * width] = blocks[part]

    def init(k, carry):
        r = pl.multiple_of(k * BLOCK, BLOCK)
        lanes = lax.broadcasted_iota(jnp.int32, (BLOCK, n), 1)
        rows = lax.broadcasted_iota(jnp.int32, (BLOCK, n), 0)
        work[pl.ds(r, BLOCK), n:] = (lanes == rows + r).astype(jnp.float32)
        return carry

    lax.fori_loop(0, count, init, 0)

    def outer(k, carry):
        r = pl.multiple_of(k * BLOCK, BLOCK)
        d = work[pl.ds(r, BLOCK), pl.ds(r, BLOCK)]
        d12 = d[:HALF, HALF:]
        first = small_inverse(d[:HALF, :HALF])
        r12 = mm(first, d12)
        second = small_inverse(d[HALF:, HALF:] - mm(r12, r12, TN))
        corner = -mm(second, mm(r12, first, TN))
        whole = jnp.concatenate(
            [
                jnp.concatenate([first, jnp.zeros((HALF, HALF), jnp.float32)], 1),
                jnp.concatenate([corner, second], 1),
            ],
            0,
        )
        work[pl.ds(r, BLOCK), :] = mm(whole, work[pl.ds(r, BLOCK), :])

        def inner(j, c):
            s = pl.multiple_of(j * BLOCK, BLOCK)
            top = work[pl.ds(r, BLOCK), :]
            left = work[pl.ds(r, BLOCK), pl.ds(s, BLOCK)]
            work[pl.ds(s, BLOCK), :] = work[pl.ds(s, BLOCK), :] - mm(left, top, TN)
            return c

        lax.fori_loop(k + 1, count, inner, 0)
        return carry

    lax.fori_loop(0, count, outer, 0)
    out[...] = work[:, n:]


def cholesky_inverse(blocks):
    n = blocks.shape[1]
    return pl.pallas_call(
        inverse_kernel,
        out_shape=jax.ShapeDtypeStruct((n, n), jnp.float32),
        in_specs=[pl.BlockSpec(memory_space=pltpu.VMEM)],
        out_specs=pl.BlockSpec(memory_space=pltpu.VMEM),
        scratch_shapes=[pltpu.VMEM((n, 2 * n), jnp.float32)],
        cost_estimate=pl.CostEstimate(
            flops=80 * n * n * n, bytes_accessed=8 * n * n, transcendentals=n
        ),
    )(blocks)


def body(own_rows, child_rows, child_dest, child_stair):
    n_front = lax.axis_size("front")
    row_count = lax.axis_size("row")
    n_col = lax.axis_size("col")
    source_rows, half_cols = child_rows.shape
    capacity = max(2, 2 * source_rows // n_front)
    col_index = lax.axis_index("col")
    global_cols = col_index * half_cols + lax.broadcasted_iota(
        jnp.int32, (source_rows, half_cols), 1
    )
    masked_rows = jnp.where(global_cols >= (child_stair * STAIR_BLK)[:, None], child_rows, 0.0)
    targets = child_dest[:, 0]
    onehot = (targets[:, None] == jnp.arange(n_front, dtype=jnp.int32)[None, :]).astype(jnp.int32)
    slot = jnp.sum((jnp.cumsum(onehot, axis=0) - onehot) * onehot, axis=1)
    eliminated = PANEL_COUNT * PANEL_COLUMNS
    parts = row_count * n_col
    sub_cap = capacity // n_col
    position = (slot % n_col) * (n_front * sub_cap) + targets * sub_cap + slot // n_col
    send_block = (
        jnp.zeros((n_front * capacity, half_cols), jnp.float32).at[position].set(masked_rows)
    )
    child = lax.all_to_all(send_block, ("col", "front"), split_axis=0, concat_axis=0, tiled=True)
    child = child.reshape(n_col, n_front * sub_cap, half_cols)
    own = lax.all_to_all(own_rows[0], "col", split_axis=0, concat_axis=0, tiled=True)
    own = own.reshape(n_col, own_rows.shape[1] // n_col, half_cols)
    products = gram(own, child, eliminated, parts)
    square_parts = eliminated * parts // (n_col * half_cols)
    square = lax.psum(products[:square_parts], ("col", "row"))
    products, square = lax.optimization_barrier((products, square))
    mine = lax.psum_scatter(products, ("col", "row"), scatter_dimension=0, tiled=True)[0]
    inverse = cholesky_inverse(square)
    factor = jnp.dot(inverse, mine, precision=HI, preferred_element_type=jnp.float32)
    factor = lax.all_to_all(
        factor, "row", split_axis=0, concat_axis=1, tiled=True
    )
    return factor[None]


def solution(mesh):
    placed = (
        P("front", "row", "col"),
        P(("front", "row"), "col"),
        P(("front", "row"), None),
        P(("front", "row")),
    )
    return jax.shard_map(
        body, mesh=mesh, in_specs=placed, out_specs=P("front", "row", "col"), check_vma=False
    )
```

time: 950 us -> 556 us (0.59)
  waiting for transfers between devices: 445 us -> 105 us
  other arithmetic: 257 us -> 10.4 us
  blocking collectives: 0 us -> 218 us
  Pallas kernels: 0 us -> 185 us
  matrix products: 142 us -> 9.28 us
  local copies, waits for them, and re-layouts: 71.8 us -> 9.57 us
    another operation x36 -> x2, other arithmetic: 241 us -> 1.41 us  [the longest x29 158 us: panel_factor(): lower_cholesky_factor = jnp.linalg.cholesky(sums_block[1])]
    all_to_all x0 -> x2, blocking collectives: none -> 218 us  [the longest x1 190 us: body(): lax.all_to_all(send_block, ('col', 'front'), split_axis=0, concat_axis=0,...]
    pallas_call x0 -> x2, Pallas kernels: none -> 185 us  [the longest x1 160 us: cholesky_inverse(): pl.pallas_call(inverse_kernel, out_shape=jax.ShapeDtypeStruct((n, n), jnp...]
    all_to_all x2 -> x1, waiting for transfers between devices: 206 us -> 26.6 us  [body(): lax.all_to_all(own_rows[0], 'col', split_axis=0, concat_axis=0, tiled=True)]
    psum x2 -> x1, waiting for transfers between devices: 238 us -> 77.9 us  [body(): square = lax.psum(products[:square_parts], ('col', 'row'))]
    another operation x33 -> x0, matrix products: 75.5 us -> none  [the longest x14 64.9 us: panel_factor(): jax.scipy.linalg.solve_triangular(lower_cholesky_factor, sums_block[0], l...]
    dot_general x3 -> x1, matrix products: 66.2 us -> 9.28 us  [body(): jnp.dot(inverse, mine, precision=HI, preferred_element_type=jnp.float32)]
    unnamed x40 -> x6, local copies, waits for them, and re-layouts: 25.4 us -> 0.01 us
  transfers between devices with their start and end apart: 4 -> 3, of which waited for: 4 -> 2; matrix products, arithmetic and copies ran while one was open for 2% -> 2% of each run, Pallas kernels for 0% -> 29%
where the time goes in v1:
time: 556 us; the launch traced here: 555 us
  blocking collectives  218 us (39%)
  Pallas kernels  185 us (33%)
  waiting for transfers between devices  105 us (19%)
  between operations  13.4 us (2%)
  other arithmetic  10.4 us (2%)
  local copies, waits for them, and re-layouts  9.57 us (2%)
  matrix products  9.28 us (2%)
    all_to_all x1, blocking collectives, body(): lax.all_to_all(send_block, ('col', 'front'), split_axis=0, concat_axis=0,...  190 us
    pallas_call x1, Pallas kernels, cholesky_inverse(): pl.pallas_call(inverse_kernel, out_shape=jax.ShapeDtypeStruct((n, n), jnp...  160 us
    psum x1, waiting for transfers between devices, body(): square = lax.psum(products[:square_parts], ('col', 'row'))  77.9 us
    all_to_all x1, blocking collectives, body(): lax.all_to_all(factor, 'row', split_axis=0, concat_axis=1, tiled=True)  28.2 us
    all_to_all x1, waiting for transfers between devices, body(): lax.all_to_all(own_rows[0], 'col', split_axis=0, concat_axis=0, tiled=True)  26.6 us
    pallas_call x1, Pallas kernels, gram(): pl.pallas_call(gram_kernel, out_shape=jax.ShapeDtypeStruct((parts, elimin...  25.6 us
  transfers between devices with their start and end apart: 3, of which 2 were waited for; matrix products, arithmetic and copies ran while one was open for 2% of the time, Pallas kernels for 29%

profile of v1, /device:TPU:0, one launch (start us, length us, event | category | flops | bytes accessed | tf_op | source)
XLA Modules:
  0.0 555.2 jit_solution(7183460651772154657)
XLA Ops:
  6.5 0.0 copy-start.1
  6.5 0.0 copy-start.2
  6.5 4.4 all-to-all-start
  10.9 0.0 all-reduce.2.cloned.1.call-start
  10.9 0.0 copy-done.1
  10.9 1.2 reduce-window.6
  12.2 0.2 slice_reduce_fusion
  12.4 0.2 reduce-window.9
  12.6 0.1 add_bitcast_fusion
  12.7 0.0 copy-done.2
  12.7 8.8 %scatter_custom_fusion = f32[1024,2048]{1,0:T(8,128)} fusion(s32[512]{0:T(512)S(1)} %bitcast.46, f32[512,2048]{1,0:T(8,128)} %param.5, f32[]{:T(128)} %constant.37.clone.1, s32[2048]{0:T(1024)S(1)} %iota_add_fusion, s32[512]{0:T(512)S(1)} %broadcast_multiply_fusion), kind=kCustom, calls=%fused_computation.1 | custom fusion | flops 2097152 | bytes 12594176 | tf_op jit(solution)/shard_map/scatter | solution.py:178
  21.6 26.6 %all-to-all-done.own_lhs.own_rhs = f32[2,192,2048]{2,1,0:T(8,128)S(1)} async-done(((f32[2,192,2048]{2,1,0:T(8,128)}), f32[2,192,2048]{2,1,0:T(8,128)S(1)}, u32[]{:S(2)}, u32[]{:S(2)}) %all-to-all-start) | async-done | bytes 3145760 | tf_op jit(solution)/shard_map/all_to_all | solution.py:182
  48.2 0.0 copy-start
  48.2 189.8 %all_to_all.31 = f32[8,128,2048]{2,1,0:T(8,128)} all-to-all(f32[8,128,2048]{2,1,0:T(8,128)} %bitcast.35), channel_id=1, replica_groups=mesh['front'=4,'row'=4,'col'=2] {'col','front'}, dimensions={0} | all-to-all | bytes 16777216 | tf_op jit(solution)/shard_map/all_to_all | solution.py:180
  238.0 0.0 copy-done
  238.0 25.6 %shard_map.46 = f32[8,1024,512]{2,1,0:T(8,128)} custom-call(f32[2,192,2048]{2,1,0:T(8,128)} %copy-done, f32[2,512,2048]{2,1,0:T(8,128)} %bitcast.36, f32[2,192,2048]{2,1,0:T(8,128)} %copy-done, f32[2,512,2048]{2,1,0:T(8,128)} %bitcast.37), custom_call_target="tpu_custom_call" | custom-call | flops 17716740096 | bytes 28311552 | tf_op jit(solution)/shard_map/pallas_call | solution.py:60
  263.6 4.6 slice.13
  268.2 0.0 all-reduce.2.cloned.1.call-update
  268.2 0.2 reduce-scatter.2.cloned.1.call-start
  268.5 77.9 %all-reduce.2.cloned.1.call-done.blocks = f32[2,1024,512]{2,1,0:T(8,128)} async-done(((f32[2,1024,512]{2,1,0:T(8,128)}), f32[2,1024,512]{2,1,0:T(8,128)}) %all-reduce.2.cloned.1.call-update) | async-done | bytes 4194320 | tf_op jit(solution)/shard_map/psum | solution.py:186
  346.4 0.0 reduce-scatter.2.cloned.1.call-update
  346.4 159.7 %shard_map.47 = f32[1024,1024]{1,0:T(8,128)} custom-call(f32[2,1024,512]{2,1,0:T(8,128)} %all-reduce.2.cloned.1.call-done.blocks), custom_call_target="tpu_custom_call" | custom-call | flops 85899345920 | bytes 8388608 | tf_op jit(solution)/shard_map/pallas_call | solution.py:147
  506.1 0.0 reduce-scatter.2.cloned.1.call-done
  506.1 9.3 %fusion.4 = f32[4,256,512]{2,1,0:T(8,128)S(1)} fusion(f32[4,256,1024]{2,1,0:T(8,128)} %bitcast.40, f32[1,1024,512]{2,1,0:T(8,128)} %reduce-scatter.2.cloned.1.call-done), kind=kOutput, calls=%fused_computation.5 | convolution fusion | flops 6442450944 | bytes 8388608 | tf_op jit(solution)/shard_map/dot_general | solution.py:190
  515.4 28.2 %all_to_all.32 = f32[4,256,512]{2,1,0:T(8,128)S(1)} all-to-all(f32[4,256,512]{2,1,0:T(8,128)S(1)} %fusion.4), channel_id=1, replica_groups=mesh['front'=4,'row'=4,'col'=2] {'row'}, dimensions={0} | all-to-all | bytes 4194304 | tf_op jit(solution)/shard_map/all_to_all | solution.py:191
  543.6 1.9 copy.5
  545.5 2.9 copy.6
  (5 shorter events, 0.1 us)
Async XLA Ops:
  6.5 4.4 copy-start.1
  6.5 6.1 %copy-start.2 = (s32[512]{0:T(512)S(1)}, s32[512]{0:T(512)}, u32[]{:S(2)}) copy-start(s32[512]{0:T(512)} %param.7) | copy-start | bytes 6148
  6.5 41.7 %all-to-all-start = ((f32[2,192,2048]{2,1,0:T(8,128)}), f32[2,192,2048]{2,1,0:T(8,128)S(1)}, u32[]{:S(2)}, u32[]{:S(2)}) async-start(f32[2,192,2048]{2,1,0:T(8,128)} %bitcast.41), calls=%async_computation | async-start | bytes 6291456 | tf_op jit(solution)/shard_map/all_to_all | solution.py:182
  10.9 335.5 %all-reduce.2.cloned.1.call-start = ((), (), s32[]{:S(2)}) async-start(), calls=%async_computation.4 | async-start | bytes 8388608 | tf_op jit(solution)/shard_map/psum | solution.py:186
  48.2 189.8 %copy-start = (f32[2,192,2048]{2,1,0:T(8,128)}, f32[2,192,2048]{2,1,0:T(8,128)S(1)}, u32[]{:S(2)}) copy-start(f32[2,192,2048]{2,1,0:T(8,128)S(1)} %all-to-all-done.own_lhs.own_rhs) | copy-start | bytes 9437188
  268.2 237.9 %reduce-scatter.2.cloned.1.call-start = ((), (), s32[]{:S(2)}) async-start(), calls=%async_computation.5 | async-start | bytes 18874368 | tf_op jit(solution)/shard_map/reduce_scatter | solution.py:188
Sparse Core Ops, SparseCore 0:
  268.4 78.0 all-reduce.1
  350.0 116.2 reduce-scatter.1

commit v2 on v1

v2 whole, which is shorter than its diff:
```python
import jax
import jax.numpy as jnp
from jax import lax
from jax.experimental import pallas as pl
from jax.experimental.pallas import tpu as pltpu
from jax.sharding import PartitionSpec as P

PANEL_COLUMNS = 512
PANEL_COUNT = 2
STAIR_BLK = 128
BLOCK = 128
HALF = 64
TILE = 256
HI = lax.Precision.HIGHEST
TN = (((0,), (0,)), ((), ()))
NN = (((1,), (0,)), ((), ()))


def mm(a, b, dims=NN):
    return lax.dot_general(a, b, dims, precision=HI, preferred_element_type=jnp.float32)


def split(x):
    hi = x.astype(jnp.bfloat16)
    return hi, (x - hi.astype(jnp.float32)).astype(jnp.bfloat16)


def dot3(a, b, dims):
    a_hi, a_lo = a
    b_hi, b_lo = b

    def dot(x, y):
        return lax.dot_general(x, y, dims, preferred_element_type=jnp.float32)

    return dot(a_lo, b_hi) + dot(a_hi, b_lo) + dot(a_hi, b_hi)


def packed_index(row, col):
    return col * (col + 1) // 2 + row


def gram_kernel(own_lhs, child_lhs, own_rhs, child_rhs, out, square, lhs_hi, lhs_lo):
    n_own = own_lhs.shape[1]
    eliminated = out.shape[1]
    width = out.shape[2]

    @pl.when(pl.program_id(0) == 0)
    def _():
        for src, start in ((own_lhs, 0), (child_lhs, n_own)):
            rows = src.shape[1]
            hi, lo = split(src[0])
            lhs_hi[start : start + rows] = hi
            lhs_lo[start : start + rows] = lo

    own_hi, own_lo = split(own_rhs[0])
    child_hi, child_lo = split(child_rhs[0])
    rhs = (jnp.concatenate([own_hi, child_hi], 0), jnp.concatenate([own_lo, child_lo], 0))
    for start in range(0, eliminated, TILE):
        cols = slice(start, start + TILE)
        out[0, cols, :] = dot3((lhs_hi[:, cols], lhs_lo[:, cols]), rhs, TN)

    for part in range(eliminated // width):

        @pl.when(pl.program_id(0) == part)
        def _():
            for local in range(width // TILE):
                col = part * (width // TILE) + local
                for row in range(col + 1):
                    square[packed_index(row, col)] = out[
                        0, row * TILE : (row + 1) * TILE, local * TILE : (local + 1) * TILE
                    ]


def gram(own, child, eliminated, parts):
    n_col, own_rows, half_cols = own.shape
    child_rows = child.shape[1]
    per = parts // n_col
    width = half_cols // per
    tiles = packed_index(0, eliminated // TILE)
    return pl.pallas_call(
        gram_kernel,
        out_shape=(
            jax.ShapeDtypeStruct((parts, eliminated, width), jnp.float32),
            jax.ShapeDtypeStruct((tiles, TILE, TILE), jnp.float32),
        ),
        grid=(parts,),
        in_specs=[
            pl.BlockSpec((1, own_rows, eliminated), lambda q: (0, 0, 0)),
            pl.BlockSpec((1, child_rows, eliminated), lambda q: (0, 0, 0)),
            pl.BlockSpec((1, own_rows, width), lambda q: (q // per, 0, q % per)),
            pl.BlockSpec((1, child_rows, width), lambda q: (q // per, 0, q % per)),
        ],
        out_specs=(
            pl.BlockSpec((1, eliminated, width), lambda q: (q, 0, 0)),
            pl.BlockSpec((tiles, TILE, TILE), lambda q: (0, 0, 0)),
        ),
        scratch_shapes=[pltpu.VMEM((own_rows + child_rows, eliminated), jnp.bfloat16)] * 2,
        cost_estimate=pl.CostEstimate(
            flops=6 * (own_rows + child_rows) * eliminated * half_cols * n_col,
            bytes_accessed=4 * (own_rows + child_rows + eliminated) * half_cols * n_col,
            transcendentals=0,
        ),
    )(own, child, own, child)


def small_inverse(block):
    lanes = lax.broadcasted_iota(jnp.int32, (HALF, HALF), 1)
    rows = lax.broadcasted_iota(jnp.int32, (HALF, HALF), 0)
    eye = (lanes == rows).astype(jnp.float32)
    both = jnp.concatenate([block, eye], 1)
    groups = [both[g * 8 : (g + 1) * 8] for g in range(HALF // 8)]
    sub = lax.broadcasted_iota(jnp.int32, (8, 1), 0)
    for j in range(HALF):
        home, inside = divmod(j, 8)
        pivot_row = groups[home][inside : inside + 1]
        pivot = pivot_row[:, j : j + 1]
        reduced = pivot_row * (1.0 / pivot)
        scaled = pivot_row * lax.rsqrt(pivot)
        for g in range(home, HALF // 8):
            column = groups[g][:, j : j + 1]
            updated = groups[g] - column * reduced
            if g == home:
                kept = jnp.where(sub == inside, scaled, groups[g])
                updated = jnp.where(sub > inside, updated, kept)
            groups[g] = updated
    return jnp.concatenate(groups, 0)[:, HALF:]


def inverse_kernel(blocks, out, work):
    n = out.shape[0]
    count = n // BLOCK
    for col in range(n // TILE):
        for row in range(col + 1):
            work[row * TILE : (row + 1) * TILE, col * TILE : (col + 1) * TILE] = blocks[
                packed_index(row, col)
            ]
    lanes = lax.broadcasted_iota(jnp.int32, (BLOCK, n), 1)
    rows = lax.broadcasted_iota(jnp.int32, (BLOCK, n), 0)

    def outer(k, carry):
        r = pl.multiple_of(k * BLOCK, BLOCK)
        d = work[pl.ds(r, BLOCK), pl.ds(r, BLOCK)]
        first = small_inverse(d[:HALF, :HALF])
        r12 = mm(first, d[:HALF, HALF:])
        second = small_inverse(d[HALF:, HALF:] - mm(r12, r12, TN))
        corner = -mm(second, mm(r12, first, TN))
        whole = jnp.concatenate(
            [
                jnp.concatenate([first, jnp.zeros((HALF, HALF), jnp.float32)], 1),
                jnp.concatenate([corner, second], 1),
            ],
            0,
        )
        here = (lanes >= r) & (lanes < r + BLOCK)
        top = jnp.where(here, (lanes == rows + r).astype(jnp.float32), work[pl.ds(r, BLOCK), :])
        top = dot3(split(whole), split(top), NN)
        work[pl.ds(r, BLOCK), :] = top

        def inner(j, c):
            s = pl.multiple_of(j * BLOCK, BLOCK)
            left = split(work[pl.ds(r, BLOCK), pl.ds(s, BLOCK)])
            right = split(work[pl.ds(r, BLOCK), :])
            kept = jnp.where(here, 0.0, work[pl.ds(s, BLOCK), :])
            work[pl.ds(s, BLOCK), :] = kept - dot3(left, right, TN)
            return c

        lax.fori_loop(k + 1, count, inner, 0)
        return carry

    lax.fori_loop(0, count, outer, 0)

    def finish(k, carry):
        r = pl.multiple_of(k * BLOCK, BLOCK)
        out[pl.ds(r, BLOCK), :] = jnp.where(lanes <= rows + r, work[pl.ds(r, BLOCK), :], 0.0)
        return carry

    lax.fori_loop(0, count, finish, 0)


def cholesky_inverse(blocks, n):
    return pl.pallas_call(
        inverse_kernel,
        out_shape=jax.ShapeDtypeStruct((n, n), jnp.float32),
        in_specs=[pl.BlockSpec(memory_space=pltpu.VMEM)],
        out_specs=pl.BlockSpec(memory_space=pltpu.VMEM),
        scratch_shapes=[pltpu.VMEM((n, n), jnp.float32)],
        cost_estimate=pl.CostEstimate(
            flops=80 * n * n * n, bytes_accessed=8 * n * n, transcendentals=n
        ),
    )(blocks)


def exchange_own(rows, n_col, col_index):
    share = rows.shape[0] // n_col
    arrived = [lax.dynamic_slice_in_dim(rows, col_index * share, share, 0)]
    for shift in range(1, n_col):
        leaving = lax.dynamic_slice_in_dim(rows, (col_index + shift) % n_col * share, share, 0)
        arrived.append(
            lax.ppermute(leaving, "col", [(i, (i + shift) % n_col) for i in range(n_col)])
        )
    blocks = []
    for source in range(n_col):
        block = arrived[0]
        for shift in range(1, n_col):
            block = jnp.where((source + shift) % n_col == col_index, arrived[shift], block)
        blocks.append(block)
    return jnp.stack(blocks)


def body(own_rows, child_rows, child_dest, child_stair):
    n_front = lax.axis_size("front")
    row_count = lax.axis_size("row")
    n_col = lax.axis_size("col")
    source_rows, half_cols = child_rows.shape
    capacity = max(2, 2 * source_rows // n_front)
    col_index = lax.axis_index("col")
    own = exchange_own(own_rows[0], n_col, col_index)
    global_cols = col_index * half_cols + lax.broadcasted_iota(
        jnp.int32, (source_rows, half_cols), 1
    )
    masked_rows = jnp.where(global_cols >= (child_stair * STAIR_BLK)[:, None], child_rows, 0.0)
    targets = child_dest[:, 0]
    onehot = (targets[:, None] == jnp.arange(n_front, dtype=jnp.int32)[None, :]).astype(jnp.int32)
    slot = jnp.sum((jnp.cumsum(onehot, axis=0) - onehot) * onehot, axis=1)
    eliminated = PANEL_COUNT * PANEL_COLUMNS
    parts = row_count * n_col
    sub_cap = capacity // n_col
    position = (slot % n_col) * (n_front * sub_cap) + targets * sub_cap + slot // n_col
    send_block = (
        jnp.zeros((n_front * capacity, half_cols), jnp.float32).at[position].set(masked_rows)
    )
    child = lax.all_to_all(send_block, ("col", "front"), split_axis=0, concat_axis=0, tiled=True)
    child = child.reshape(n_col, n_front * sub_cap, half_cols)
    products, square = gram(own, child, eliminated, parts)
    square = lax.psum(square, ("col", "row"))
    products, square = lax.optimization_barrier((products, square))
    mine = lax.psum_scatter(products, ("col", "row"), scatter_dimension=0, tiled=True)[0]
    inverse = cholesky_inverse(square, eliminated)
    factor = jnp.dot(
        inverse, mine, precision=lax.Precision.HIGH, preferred_element_type=jnp.float32
    )
    factor = lax.all_to_all(
        factor, "row", split_axis=0, concat_axis=1, tiled=True
    )
    return factor[None]


def solution(mesh):
    placed = (
        P("front", "row", "col"),
        P(("front", "row"), "col"),
        P(("front", "row"), None),
        P(("front", "row")),
    )
    return jax.shard_map(
        body, mesh=mesh, in_specs=placed, out_specs=P("front", "row", "col"), check_vma=False
    )
```

time: 556 us -> 466 us (0.84)
  blocking collectives: 218 us -> 28.2 us
  waiting for transfers between devices: 105 us -> 247 us
  Pallas kernels: 185 us -> 138 us
  other arithmetic: 10.4 us -> 16.7 us
    all_to_all x1 -> x0, blocking collectives: 190 us -> none  [body(): lax.all_to_all(send_block, ('col', 'front'), split_axis=0, concat_axis=0,...]
    ppermute x0 -> x1, waiting for transfers between devices: none -> 77.8 us  [exchange_own(): lax.ppermute(leaving, 'col', [(i, (i + shift) % n_col) for i in range(n_c...]
    all_to_all x1, waiting for transfers between devices: 26.6 us -> 99.5 us  [body(): lax.all_to_all(send_block, ('col', 'front'), split_axis=0, concat_axis=0,...]
    pallas_call x1, Pallas kernels: 160 us -> 111 us  [cholesky_inverse(): pl.pallas_call(inverse_kernel, out_shape=jax.ShapeDtypeStruct((n, n), jnp...]
    psum x1, waiting for transfers between devices: 77.9 us -> 61.8 us  [body(): square = lax.psum(square, ('col', 'row'))]
    reduce_scatter x1, waiting for transfers between devices: 0.01 us -> 8.23 us  [body(): lax.psum_scatter(products, ('col', 'row'), scatter_dimension=0, tiled=True)]
  transfers between devices with their start and end apart: 3 -> 4, of which waited for: 2 -> 4; matrix products, arithmetic and copies ran while one was open for 2% -> 1% of each run, Pallas kernels for 29% -> 24%
where the time goes in v2:
time: 466 us
  waiting for transfers between devices  247 us (53%)
  Pallas kernels  138 us (30%)
  blocking collectives  28.2 us (6%)
  other arithmetic  16.7 us (4%)
  between operations  13.5 us (3%)
  starting transfers between devices  9.79 us (2%)
  local copies, waits for them, and re-layouts  6.22 us (1%)
  matrix products  5.94 us (1%)
    pallas_call x1, Pallas kernels, cholesky_inverse(): pl.pallas_call(inverse_kernel, out_shape=jax.ShapeDtypeStruct((n, n), jnp...  111 us
    all_to_all x1, waiting for transfers between devices, body(): lax.all_to_all(send_block, ('col', 'front'), split_axis=0, concat_axis=0,...  99.5 us
    ppermute x1, waiting for transfers between devices, exchange_own(): lax.ppermute(leaving, 'col', [(i, (i + shift) % n_col) for i in range(n_c...  77.8 us
    psum x1, waiting for transfers between devices, body(): square = lax.psum(square, ('col', 'row'))  61.8 us
    all_to_all x1, blocking collectives, body(): lax.all_to_all(factor, 'row', split_axis=0, concat_axis=1, tiled=True)  28.2 us
    pallas_call x1, Pallas kernels, gram(): pl.pallas_call(gram_kernel, out_shape=(jax.ShapeDtypeStruct((parts, elimi...  26.7 us
  transfers between devices with their start and end apart: 4, of which 4 were waited for; matrix products, arithmetic and copies ran while one was open for 1% of the time, Pallas kernels for 24%

profile of v2, /device:TPU:0, one launch (start us, length us, event | category | flops | bytes accessed | tf_op | source)
XLA Modules:
  0.0 465.6 jit_solution(3665188823837694823)
XLA Ops:
  6.5 0.7 broadcast_multiply_fusion
  7.2 0.7 fusion.14
  7.9 1.2 reduce-window.6
  9.1 0.2 slice_reduce_fusion
  9.3 0.2 reduce-window.9
  9.5 0.1 add_bitcast_fusion
  9.6 0.7 fusion.13
  10.3 0.7 compare_select_fusion
  11.0 8.8 %scatter_custom_fusion = f32[1024,2048]{1,0:T(8,128)} fusion(s32[512]{0:T(512)S(1)} %bitcast.55, f32[512,2048]{1,0:T(8,128)} %param.5, f32[]{:T(128)} %constant.54.clone.1, s32[2048]{0:T(1024)S(1)} %iota_add_fusion, s32[512]{0:T(512)S(1)} %broadcast_multiply_fusion), kind=kCustom, calls=%fused_computation.1 | custom fusion | flops 2097152 | bytes 12594176 | tf_op jit(solution)/shard_map/scatter | solution.py:230
  19.8 0.0 copy-start
  19.8 7.6 %all-to-all-start = ((f32[8,128,2048]{2,1,0:T(8,128)}), f32[8,128,2048]{2,1,0:T(8,128)}, u32[]{:S(2)}, u32[]{:S(2)}) async-start(f32[8,128,2048]{2,1,0:T(8,128)} %bitcast.47), calls=%async_computation | async-start | bytes 16777216 | tf_op jit(solution)/shard_map/all_to_all | solution.py:232
  27.4 0.0 all-reduce.2.cloned.1.call-start
  27.5 0.0 copy-done
  27.5 1.3 dynamic-slice_bitcast_fusion
  28.7 2.0 collective-permute-start
  30.7 77.8 %collective-permute-done = f32[192,2048]{1,0:T(8,128)} collective-permute-done((f32[192,2048]{1,0:T(8,128)}, f32[192,2048]{1,0:T(8,128)}, u32[]{:S(2)}, u32[]{:S(2)}) %collective-permute-start) | collective-permute-done | bytes 1572896 | tf_op jit(solution)/shard_map/ppermute | solution.py:199
  108.5 1.6 fusion.9
  110.2 2.0 pad_maximum_fusion.own_lhs.own_rhs
  112.1 99.5 %all-to-all-done = f32[8,128,2048]{2,1,0:T(8,128)} async-done(((f32[8,128,2048]{2,1,0:T(8,128)}), f32[8,128,2048]{2,1,0:T(8,128)}, u32[]{:S(2)}, u32[]{:S(2)}) %all-to-all-start) | async-done | bytes 8388640 | tf_op jit(solution)/shard_map/all_to_all | solution.py:232
  211.6 26.7 %shard_map.46 = (f32[8,1024,512]{2,1,0:T(8,128)}, f32[10,256,256]{2,1,0:T(8,128)}) custom-call(f32[2,192,2048]{2,1,0:T(8,128)} %pad_maximum_fusion.own_lhs.own_rhs, f32[2,512,2048]{2,1,0:T(8,128)} %bitcast.10.child_lhs.child_rhs, f32[2,192,2048]{2,1,0:T(8,128)} %pad_maximum_fusion.own_lhs.own_rhs, f32[2,512,2048]{2,1,0:T(8,128)} %bitcast.10.child_lhs.child_rhs), custom_call_target="tpu_custom_call" | custom-call | flops 17716740096 | bytes 28311552 | tf_op jit(solution)/shard_map/pallas_call | solution.py:80
  238.3 0.0 all-reduce.2.cloned.1.call-update
  238.3 0.2 reduce-scatter.2.cloned.1.call-start
  238.6 61.8 %all-reduce.2.cloned.1.call-done.blocks = f32[10,256,256]{2,1,0:T(8,128)} async-done(((f32[10,256,256]{2,1,0:T(8,128)}), f32[10,256,256]{2,1,0:T(8,128)}) %all-reduce.2.cloned.1.call-update) | async-done | bytes 2621456 | tf_op jit(solution)/shard_map/psum | solution.py:235
  300.4 0.0 reduce-scatter.2.cloned.1.call-update
  300.4 111.2 %shard_map.47 = f32[1024,1024]{1,0:T(8,128)} custom-call(f32[10,256,256]{2,1,0:T(8,128)} %all-reduce.2.cloned.1.call-done.blocks), custom_call_target="tpu_custom_call" | custom-call | flops 85899345920 | bytes 8388608 | tf_op jit(solution)/shard_map/pallas_call | solution.py:181
  411.6 8.2 %reduce-scatter.2.cloned.1.call-done = f32[1,1024,512]{2,1,0:T(8,128)} async-done(((f32[8,1024,512]{2,1,0:T(8,128)}), f32[1,1024,512]{2,1,0:T(8,128)}) %reduce-scatter.2.cloned.1.call-update) | async-done | bytes 2097168 | tf_op jit(solution)/shard_map/reduce_scatter | solution.py:237
  419.8 5.9 %fusion.4 = f32[4,256,512]{2,1,0:T(8,128)S(1)} fusion(f32[4,256,1024]{2,1,0:T(8,128)} %bitcast.50, f32[1,1024,512]{2,1,0:T(8,128)} %reduce-scatter.2.cloned.1.call-done), kind=kOutput, calls=%fused_computation.6 | convolution fusion | flops 3221225472 | bytes 8388608 | tf_op jit(solution)/shard_map/dot_general | solution.py:239
  425.8 28.2 %all_to_all.22 = f32[4,256,512]{2,1,0:T(8,128)S(1)} all-to-all(f32[4,256,512]{2,1,0:T(8,128)S(1)} %fusion.4), channel_id=1, replica_groups=mesh['front'=4,'row'=4,'col'=2] {'row'}, dimensions={0} | all-to-all | bytes 4194304 | tf_op jit(solution)/shard_map/all_to_all | solution.py:242
  454.0 1.9 copy.5
  455.9 2.9 copy.6
  (1 shorter events, 0.0 us)
Async XLA Ops:
  19.8 7.6 %copy-start = (f32[1,384,2048]{2,1,0:T(8,128)S(1)}, f32[1,384,2048]{2,1,0:T(8,128)}, u32[]{:S(2)}) copy-start(f32[1,384,2048]{2,1,0:T(8,128)} %param.4) | copy-start | bytes 9437188
  19.8 191.7 %all-to-all-start = ((f32[8,128,2048]{2,1,0:T(8,128)}), f32[8,128,2048]{2,1,0:T(8,128)}, u32[]{:S(2)}, u32[]{:S(2)}) async-start(f32[8,128,2048]{2,1,0:T(8,128)} %bitcast.47), calls=%async_computation | async-start | bytes 16777216 | tf_op jit(solution)/shard_map/all_to_all | solution.py:232
  27.4 273.0 %all-reduce.2.cloned.1.call-start = ((), (), s32[]{:S(2)}) async-start(), calls=%async_computation.3 | async-start | bytes 5242880 | tf_op jit(solution)/shard_map/psum | solution.py:235
  28.7 79.8 %collective-permute-start = (f32[192,2048]{1,0:T(8,128)}, f32[192,2048]{1,0:T(8,128)}, u32[]{:S(2)}, u32[]{:S(2)}) collective-permute-start(f32[192,2048]{1,0:T(8,128)} %dynamic-slice_bitcast_fusion), channel_id=1, source_target_pairs={{0,1},{1,0},{2,3},{3,2},{4,5},{5,4},{6,7},{7,6},{8,9},{9,8},{10,11... | collective-permute-start | bytes 4718600 | tf_op jit(solution)/shard_map/ppermute | solution.py:199
  238.3 181.5 %reduce-scatter.2.cloned.1.call-start = ((), (), s32[]{:S(2)}) async-start(), calls=%async_computation.4 | async-start | bytes 18874368 | tf_op jit(solution)/shard_map/reduce_scatter | solution.py:237
Sparse Core Ops, SparseCore 0:
  238.5 61.8 all-reduce.1
  303.9 115.8 reduce-scatter.1

commit v3 on v2

--- a/solution.py
+++ b/solution.py
@@ -39,10 +39,11 @@
     return col * (col + 1) // 2 + row
 
 
-def gram_kernel(own_lhs, child_lhs, own_rhs, child_rhs, out, square, lhs_hi, lhs_lo):
+def gram_kernel(own_lhs, child_lhs, *refs):
+    *rhs_refs, out, square, lhs_hi, lhs_lo = refs
     n_own = own_lhs.shape[1]
     eliminated = out.shape[1]
-    width = out.shape[2]
+    tiles = eliminated // TILE
 
     @pl.when(pl.program_id(0) == 0)
     def _():
@@ -52,46 +53,54 @@
             lhs_hi[start : start + rows] = hi
             lhs_lo[start : start + rows] = lo
 
-    own_hi, own_lo = split(own_rhs[0])
-    child_hi, child_lo = split(child_rhs[0])
-    rhs = (jnp.concatenate([own_hi, child_hi], 0), jnp.concatenate([own_lo, child_lo], 0))
-    for start in range(0, eliminated, TILE):
-        cols = slice(start, start + TILE)
-        out[0, cols, :] = dot3((lhs_hi[:, cols], lhs_lo[:, cols]), rhs, TN)
-
-    for part in range(eliminated // width):
-
-        @pl.when(pl.program_id(0) == part)
+    half = len(rhs_refs) // 2
+    own_rhs = jnp.concatenate([ref[0] for ref in rhs_refs[:half]], 1)
+    child_rhs = jnp.concatenate([ref[0] for ref in rhs_refs[half:]], 1)
+    rhs = split(jnp.concatenate([own_rhs, child_rhs], 0))
+
+    def lhs(row):
+        cols = slice(row * TILE, (row + 1) * TILE)
+        return lhs_hi[:, cols], lhs_lo[:, cols]
+
+    for row in range(tiles):
+        out[0, row * TILE : (row + 1) * TILE, :] = dot3(lhs(row), rhs, TN)
+
+    for col in range(tiles):
+
+        @pl.when(pl.program_id(0) == col)
         def _():
-            for local in range(width // TILE):
-                col = part * (width // TILE) + local
-                for row in range(col + 1):
-                    square[packed_index(row, col)] = out[
-                        0, row * TILE : (row + 1) * TILE, local * TILE : (local + 1) * TILE
-                    ]
+            for row in range(col + 1):
+                square[packed_index(row, col)] = dot3(lhs(row), lhs(col), TN)
 
 
 def gram(own, child, eliminated, parts):
     n_col, own_rows, half_cols = own.shape
     child_rows = child.shape[1]
-    per = parts // n_col
-    width = half_cols // per
+    widths = [(half_cols - (eliminated if c == 0 else 0)) // parts for c in range(n_col)]
+    skips = [eliminated // widths[0]] + [0] * (n_col - 1)
     tiles = packed_index(0, eliminated // TILE)
+
+    def pieces(rows):
+        return [
+            pl.BlockSpec((1, rows, widths[c]), lambda q, c=c: (c, 0, skips[c] + q))
+            for c in range(n_col)
+        ]
+
     return pl.pallas_call(
         gram_kernel,
         out_shape=(
-            jax.ShapeDtypeStruct((parts, eliminated, width), jnp.float32),
+            jax.ShapeDtypeStruct((parts, eliminated, sum(widths)), jnp.float32),
             jax.ShapeDtypeStruct((tiles, TILE, TILE), jnp.float32),
         ),
         grid=(parts,),
         in_specs=[
             pl.BlockSpec((1, own_rows, eliminated), lambda q: (0, 0, 0)),
             pl.BlockSpec((1, child_rows, eliminated), lambda q: (0, 0, 0)),
-            pl.BlockSpec((1, own_rows, width), lambda q: (q // per, 0, q % per)),
-            pl.BlockSpec((1, child_rows, width), lambda q: (q // per, 0, q % per)),
-        ],
+        ]
+        + pieces(own_rows)
+        + pieces(child_rows),
         out_specs=(
-            pl.BlockSpec((1, eliminated, width), lambda q: (q, 0, 0)),
+            pl.BlockSpec((1, eliminated, sum(widths)), lambda q: (q, 0, 0)),
             pl.BlockSpec((tiles, TILE, TILE), lambda q: (0, 0, 0)),
         ),
         scratch_shapes=[pltpu.VMEM((own_rows + child_rows, eliminated), jnp.bfloat16)] * 2,
@@ -100,7 +109,7 @@
             bytes_accessed=4 * (own_rows + child_rows + eliminated) * half_cols * n_col,
             transcendentals=0,
         ),
-    )(own, child, own, child)
+    )(own, child, *([own] * n_col), *([child] * n_col))
 
 
 def small_inverse(block):
@@ -108,25 +117,46 @@
     rows = lax.broadcasted_iota(jnp.int32, (HALF, HALF), 0)
     eye = (lanes == rows).astype(jnp.float32)
     both = jnp.concatenate([block, eye], 1)
-    groups = [both[g * 8 : (g + 1) * 8] for g in range(HALF // 8)]
-    sub = lax.broadcasted_iota(jnp.int32, (8, 1), 0)
-    for j in range(HALF):
-        home, inside = divmod(j, 8)
-        pivot_row = groups[home][inside : inside + 1]
-        pivot = pivot_row[:, j : j + 1]
-        reduced = pivot_row * (1.0 / pivot)
-        scaled = pivot_row * lax.rsqrt(pivot)
-        for g in range(home, HALF // 8):
-            column = groups[g][:, j : j + 1]
-            updated = groups[g] - column * reduced
-            if g == home:
-                kept = jnp.where(sub == inside, scaled, groups[g])
-                updated = jnp.where(sub > inside, updated, kept)
-            groups[g] = updated
+    count = HALF // 8
+    groups = [both[g * 8 : (g + 1) * 8] for g in range(count)]
+    sub = lax.broadcasted_iota(jnp.int32, (8, 2 * HALF), 0)
+
+    def column_of(g, j):
+        return jnp.broadcast_to(groups[g][:, j : j + 1], (8, 2 * HALF))
+
+    def row_of(x, s):
+        return jnp.broadcast_to(x[s : s + 1], x.shape)
+
+    for home in range(count):
+        first = home * 8
+        below = [[column_of(g, first + s) for s in range(8)] for g in range(home + 1, count)]
+        columns = [column_of(home, first + s) for s in range(8)]
+        solved = forward = groups[home]
+        pivots = columns[0]
+        for s in range(8):
+            column = columns[s]
+            pivot = row_of(column, s)
+            inverse = 1.0 / pivot
+            pivots = jnp.where(sub == s, pivot, pivots)
+            forward = jnp.where(
+                sub > s, forward - column * (row_of(forward, s) * inverse), forward
+            )
+            scaled = row_of(solved, s) * inverse
+            solved = jnp.where(sub == s, scaled, solved - column * scaled)
+            for t in range(s + 1, 8):
+                scaled = row_of(columns[t], s) * inverse
+                columns[t] = jnp.where(sub == s, scaled, columns[t] - column * scaled)
+        groups[home] = forward * lax.rsqrt(pivots)
+        spread = [row_of(solved, s) for s in range(8)]
+        for g in range(home + 1, count):
+            terms = [below[g - home - 1][s] * spread[s] for s in range(8)]
+            while len(terms) > 1:
+                terms = [terms[i] + terms[i + 1] for i in range(0, len(terms), 2)]
+            groups[g] = groups[g] - terms[0]
     return jnp.concatenate(groups, 0)[:, HALF:]
 
 
-def inverse_kernel(blocks, out, work):
+def inverse_kernel(blocks, out, upper, work):
     n = out.shape[0]
     count = n // BLOCK
     for col in range(n // TILE):
@@ -152,9 +182,10 @@
             0,
         )
         here = (lanes >= r) & (lanes < r + BLOCK)
-        top = jnp.where(here, (lanes == rows + r).astype(jnp.float32), work[pl.ds(r, BLOCK), :])
-        top = dot3(split(whole), split(top), NN)
+        top = dot3(split(whole), split(work[pl.ds(r, BLOCK), :]), NN)
+        upper[pl.ds(r, BLOCK), :] = jnp.where(lanes >= rows + r, top, 0.0)
         work[pl.ds(r, BLOCK), :] = top
+        work[pl.ds(r, BLOCK), pl.ds(r, BLOCK)] = whole
 
         def inner(j, c):
             s = pl.multiple_of(j * BLOCK, BLOCK)
@@ -180,9 +211,9 @@
 def cholesky_inverse(blocks, n):
     return pl.pallas_call(
         inverse_kernel,
-        out_shape=jax.ShapeDtypeStruct((n, n), jnp.float32),
+        out_shape=(jax.ShapeDtypeStruct((n, n), jnp.float32),) * 2,
         in_specs=[pl.BlockSpec(memory_space=pltpu.VMEM)],
-        out_specs=pl.BlockSpec(memory_space=pltpu.VMEM),
+        out_specs=(pl.BlockSpec(memory_space=pltpu.VMEM),) * 2,
         scratch_shapes=[pltpu.VMEM((n, n), jnp.float32)],
         cost_estimate=pl.CostEstimate(
             flops=80 * n * n * n, bytes_accessed=8 * n * n, transcendentals=n
@@ -235,14 +266,27 @@
     square = lax.psum(square, ("col", "row"))
     products, square = lax.optimization_barrier((products, square))
     mine = lax.psum_scatter(products, ("col", "row"), scatter_dimension=0, tiled=True)[0]
-    inverse = cholesky_inverse(square, eliminated)
+    inverse, upper = cholesky_inverse(square, eliminated)
     factor = jnp.dot(
         inverse, mine, precision=lax.Precision.HIGH, preferred_element_type=jnp.float32
     )
-    factor = lax.all_to_all(
-        factor, "row", split_axis=0, concat_axis=1, tiled=True
-    )
-    return factor[None]
+    share = eliminated // parts
+    part = col_index * row_count + lax.axis_index("row")
+    piece = lax.dynamic_slice_in_dim(upper, part * share, share, 1)
+    width = half_cols // parts
+    factor = jnp.concatenate([piece, factor], 1)
+    blocks = [factor[:, c * width : (c + 1) * width] for c in range(n_col)]
+    factor = jnp.stack(blocks).reshape(parts, eliminated // row_count, width)
+    factor = lax.all_to_all(factor, ("col", "row"), split_axis=0, concat_axis=0, tiled=True)
+    plain = factor.transpose(1, 0, 2).reshape(-1, half_cols)
+    mixed = jnp.concatenate(
+        [
+            factor[:, :, :share].transpose(1, 0, 2).reshape(-1, eliminated),
+            factor[:, :, share:].transpose(1, 0, 2).reshape(-1, half_cols - eliminated),
+        ],
+        1,
+    )
+    return jnp.where(col_index == 0, mixed, plain)[None]
 
 
 def solution(mesh):

time: 466 us -> 458 us (0.983)
  Pallas kernels: 138 us -> 93 us
  waiting for transfers between devices: 247 us -> 271 us
  local copies, waits for them, and re-layouts: 6.22 us -> 15.1 us
    pallas_call x1, Pallas kernels: 111 us -> 62.3 us  [cholesky_inverse(): pl.pallas_call(inverse_kernel, out_shape=(jax.ShapeDtypeStruct((n, n), jn...]
    reduce_scatter x1, waiting for transfers between devices: 8.23 us -> 32 us  [body(): lax.psum_scatter(products, ('col', 'row'), scatter_dimension=0, tiled=True)]
    transpose x0 -> x4, local copies, waits for them, and re-layouts: none -> 7.23 us  [the longest x1 2.97 us: body(): factor[:, :, share:].transpose(1, 0, 2).reshape(-1, half_cols - eliminated)]
  transfers between devices with their start and end apart: 4 -> 4, of which waited for: 4 -> 4; matrix products, arithmetic and copies ran while one was open for 1% -> 1% of each run, Pallas kernels for 24% -> 14%
where the time goes in v3:
time: 458 us; the launch traced here: 457 us
  waiting for transfers between devices  271 us (59%)
  Pallas kernels  93 us (20%)
  blocking collectives  29.1 us (6%)
  other arithmetic  19.7 us (4%)
  local copies, waits for them, and re-layouts  15.1 us (3%)
  between operations  13.5 us (3%)
  starting transfers between devices  9.83 us (2%)
  matrix products  5.68 us (1%)
    all_to_all x1, waiting for transfers between devices, body(): lax.all_to_all(send_block, ('col', 'front'), split_axis=0, concat_axis=0,...  99.5 us
    ppermute x1, waiting for transfers between devices, exchange_own(): lax.ppermute(leaving, 'col', [(i, (i + shift) % n_col) for i in range(n_c...  77.8 us
    pallas_call x1, Pallas kernels, cholesky_inverse(): pl.pallas_call(inverse_kernel, out_shape=(jax.ShapeDtypeStruct((n, n), jn...  62.3 us
    psum x1, waiting for transfers between devices, body(): square = lax.psum(square, ('col', 'row'))  61.7 us
    reduce_scatter x1, waiting for transfers between devices, body(): lax.psum_scatter(products, ('col', 'row'), scatter_dimension=0, tiled=True)  32 us
    pallas_call x1, Pallas kernels, gram(): pl.pallas_call(gram_kernel, out_shape=(jax.ShapeDtypeStruct((parts, elimi...  30.8 us
    all_to_all x1, blocking collectives, body(): lax.all_to_all(factor, ('col', 'row'), split_axis=0, concat_axis=0, tiled...  29.1 us
  transfers between devices with their start and end apart: 4, of which 4 were waited for; matrix products, arithmetic and copies ran while one was open for 1% of the time, Pallas kernels for 14%

profile of v3, /device:TPU:0, one launch (start us, length us, event | category | flops | bytes accessed | tf_op | source)
XLA Modules:
  0.0 457.1 jit_solution(1926673471623997604)
XLA Ops:
  6.5 0.7 broadcast_multiply_fusion
  7.2 0.7 fusion.15
  7.9 1.2 reduce-window.6
  9.1 0.2 slice_reduce_fusion
  9.3 0.2 reduce-window.9
  9.5 0.1 add_bitcast_fusion
  9.6 0.7 fusion.14
  10.3 0.7 compare_select_fusion
  11.0 8.8 %scatter_custom_fusion = f32[1024,2048]{1,0:T(8,128)} fusion(s32[512]{0:T(512)S(1)} %bitcast.60, f32[512,2048]{1,0:T(8,128)} %param.5, f32[]{:T(128)} %constant.60.clone.1, s32[2048]{0:T(1024)S(1)} %iota_add_fusion, s32[512]{0:T(512)S(1)} %broadcast_multiply_fusion), kind=kCustom, calls=%fused_computation.1 | custom fusion | flops 2097152 | bytes 12594176 | tf_op jit(solution)/shard_map/scatter | solution.py:261
  19.8 0.0 copy-start.1
  19.8 7.6 %all-to-all-start = ((f32[8,128,2048]{2,1,0:T(8,128)}), f32[8,128,2048]{2,1,0:T(8,128)}, u32[]{:S(2)}, u32[]{:S(2)}) async-start(f32[8,128,2048]{2,1,0:T(8,128)} %bitcast.53), calls=%async_computation | async-start | bytes 16777216 | tf_op jit(solution)/shard_map/all_to_all | solution.py:263
  27.4 0.2 all-reduce.2.cloned.1.call-start
  27.7 0.0 copy-done.1
  27.7 1.3 dynamic-slice_bitcast_fusion
  28.9 1.8 collective-permute-start
  30.7 77.8 %collective-permute-done = f32[192,2048]{1,0:T(8,128)} collective-permute-done((f32[192,2048]{1,0:T(8,128)}, f32[192,2048]{1,0:T(8,128)}, u32[]{:S(2)}, u32[]{:S(2)}) %collective-permute-start) | collective-permute-done | bytes 1572896 | tf_op jit(solution)/shard_map/ppermute | solution.py:230
  108.5 1.6 fusion.9
  110.2 1.9 pad_maximum_fusion.own_lhs.refs_0_.refs_1_
  112.1 99.5 %all-to-all-done = f32[8,128,2048]{2,1,0:T(8,128)} async-done(((f32[8,128,2048]{2,1,0:T(8,128)}), f32[8,128,2048]{2,1,0:T(8,128)}, u32[]{:S(2)}, u32[]{:S(2)}) %all-to-all-start) | async-done | bytes 8388640 | tf_op jit(solution)/shard_map/all_to_all | solution.py:263
  211.6 30.8 %shard_map.46 = (f32[8,1024,384]{2,1,0:T(8,128)}, f32[10,256,256]{2,1,0:T(8,128)}) custom-call(f32[2,192,2048]{2,1,0:T(8,128)} %pad_maximum_fusion.own_lhs.refs_0_.refs_1_, f32[2,512,2048]{2,1,0:T(8,128)} %bitcast.10.child_lhs.refs_2_.refs_3_, f32[2,192,2048]{2,1,0:T(8,128)} %pad_maximum_fusion.own_lhs.refs_0_.refs_1_, ...), custom_call_target="tpu_custom_call" | custom-call | flops 17716740096 | bytes 28311552 | tf_op jit(solution)/shard_map/pallas_call | solution.py:89
  242.3 0.0 all-reduce.2.cloned.1.call-update
  242.4 0.3 reduce-scatter.2.cloned.1.call-start
  242.6 61.7 %all-reduce.2.cloned.1.call-done.blocks = f32[10,256,256]{2,1,0:T(8,128)} async-done(((f32[10,256,256]{2,1,0:T(8,128)}), f32[10,256,256]{2,1,0:T(8,128)}) %all-reduce.2.cloned.1.call-update) | async-done | bytes 2621456 | tf_op jit(solution)/shard_map/psum | solution.py:266
  304.4 0.0 reduce-scatter.2.cloned.1.call-update
  304.4 62.3 %shard_map.47 = (f32[1024,1024]{1,0:T(8,128)}, f32[1024,1024]{1,0:T(8,128)}) custom-call(f32[10,256,256]{2,1,0:T(8,128)} %all-reduce.2.cloned.1.call-done.blocks), custom_call_target="tpu_custom_call" | custom-call | flops 85899345920 | bytes 8388608 | tf_op jit(solution)/shard_map/pallas_call | solution.py:212
  366.7 1.1 constant_dynamic-slice_fusion
  367.8 32.0 %reduce-scatter.2.cloned.1.call-done = f32[1,1024,384]{2,1,0:T(8,128)} async-done(((f32[8,1024,384]{2,1,0:T(8,128)}), f32[1,1024,384]{2,1,0:T(8,128)}) %reduce-scatter.2.cloned.1.call-update) | async-done | bytes 1572880 | tf_op jit(solution)/shard_map/reduce_scatter | solution.py:268
  399.8 5.7 %fusion.7 = f32[1024,384]{1,0:T(8,128)S(1)} fusion(f32[1024,1024]{1,0:T(8,128)} %get-tuple-element.15, f32[1,1024,384]{2,1,0:T(8,128)} %reduce-scatter.2.cloned.1.call-done), kind=kOutput, calls=%fused_computation.11 | convolution fusion | flops 2415919104 | bytes 7340032 | tf_op jit(solution)/shard_map/dot_general | solution.py:270
  405.5 0.2 fusion.11
  405.6 0.1 pad_maximum_fusion.1
  405.8 29.1 %all_to_all.14 = f32[8,256,256]{2,1,0:T(8,128)S(1)} all-to-all(f32[8,256,256]{2,1,0:T(8,128)S(1)} %bitcast.55), channel_id=1, replica_groups=mesh['front'=4,'row'=4,'col'=2] {'col','row'}, dimensions={0} | all-to-all | bytes 4194304 | tf_op jit(solution)/shard_map/all_to_all | solution.py:280
  434.9 2.5 copy.10
  437.4 2.7 reshape.148
  440.2 1.1 slice_bitcast_fusion.1
  441.3 0.6 copy.8
  441.9 0.2 concatenate.18
  442.1 0.0 copy-start
  442.1 3.0 copy.9
  445.0 2.4 concatenate.19
  447.4 0.0 copy-done
  447.4 2.8 maximum_select_fusion
  (1 shorter events, 0.0 us)
Async XLA Ops:
  19.8 7.8 %copy-start.1 = (f32[1,384,2048]{2,1,0:T(8,128)S(1)}, f32[1,384,2048]{2,1,0:T(8,128)}, u32[]{:S(2)}) copy-start(f32[1,384,2048]{2,1,0:T(8,128)} %param.4) | copy-start | bytes 9437188
  19.8 191.7 %all-to-all-start = ((f32[8,128,2048]{2,1,0:T(8,128)}), f32[8,128,2048]{2,1,0:T(8,128)}, u32[]{:S(2)}, u32[]{:S(2)}) async-start(f32[8,128,2048]{2,1,0:T(8,128)} %bitcast.53), calls=%async_computation | async-start | bytes 16777216 | tf_op jit(solution)/shard_map/all_to_all | solution.py:263
  27.4 277.0 %all-reduce.2.cloned.1.call-start = ((), (), s32[]{:S(2)}) async-start(), calls=%async_computation.3 | async-start | bytes 5242880 | tf_op jit(solution)/shard_map/psum | solution.py:266
  28.9 79.6 %collective-permute-start = (f32[192,2048]{1,0:T(8,128)}, f32[192,2048]{1,0:T(8,128)}, u32[]{:S(2)}, u32[]{:S(2)}) collective-permute-start(f32[192,2048]{1,0:T(8,128)} %dynamic-slice_bitcast_fusion), channel_id=1, source_target_pairs={{0,1},{1,0},{2,3},{3,2},{4,5},{5,4},{6,7},{7,6},{8,9},{9,8},{10,11... | collective-permute-start | bytes 4718600 | tf_op jit(solution)/shard_map/ppermute | solution.py:230
  242.4 157.4 %reduce-scatter.2.cloned.1.call-start = ((), (), s32[]{:S(2)}) async-start(), calls=%async_computation.4 | async-start | bytes 14155776 | tf_op jit(solution)/shard_map/reduce_scatter | solution.py:268
  442.1 5.3 %copy-start = (f32[1,256,2048]{2,1,0:T(8,128)S(1)}, f32[1,256,2048]{2,1,0:T(8,128)}, u32[]{:S(2)}) copy-start(f32[1,256,2048]{2,1,0:T(8,128)} %reshape.148) | copy-start | bytes 6291460
Sparse Core Ops, SparseCore 0:
  242.5 61.8 all-reduce.1
  307.9 91.8 reduce-scatter.1

commit v4 on v3

--- a/solution.py
+++ b/solution.py
@@ -238,6 +238,31 @@
     return jnp.stack(blocks)
 
 
+def assemble_kernel(col_ref, piece, out):
+    out[...] = piece[0]
+
+
+def assemble(factor, col_index, share):
+    parts, rows, width = factor.shape
+    halves = width // share
+
+    def source(b, col_ref):
+        first = col_ref[0] == 0
+        part = jnp.where(first, b % parts, b // halves)
+        return part, 0, jnp.where(first, b // parts, b % halves)
+
+    return pl.pallas_call(
+        assemble_kernel,
+        out_shape=jax.ShapeDtypeStruct((rows, parts * width), jnp.float32),
+        grid_spec=pltpu.PrefetchScalarGridSpec(
+            num_scalar_prefetch=1,
+            grid=(parts * halves,),
+            in_specs=[pl.BlockSpec((1, rows, share), source)],
+            out_specs=pl.BlockSpec((rows, share), lambda b, col_ref: (0, b)),
+        ),
+    )(col_index.reshape(1).astype(jnp.int32), factor)
+
+
 def body(own_rows, child_rows, child_dest, child_stair):
     n_front = lax.axis_size("front")
     row_count = lax.axis_size("row")
@@ -278,15 +303,7 @@
     blocks = [factor[:, c * width : (c + 1) * width] for c in range(n_col)]
     factor = jnp.stack(blocks).reshape(parts, eliminated // row_count, width)
     factor = lax.all_to_all(factor, ("col", "row"), split_axis=0, concat_axis=0, tiled=True)
-    plain = factor.transpose(1, 0, 2).reshape(-1, half_cols)
-    mixed = jnp.concatenate(
-        [
-            factor[:, :, :share].transpose(1, 0, 2).reshape(-1, eliminated),
-            factor[:, :, share:].transpose(1, 0, 2).reshape(-1, half_cols - eliminated),
-        ],
-        1,
-    )
-    return jnp.where(col_index == 0, mixed, plain)[None]
+    return assemble(factor, col_index, share)[None]
 
 
 def solution(mesh):

time: 458 us -> 452 us (0.987)
  local copies, waits for them, and re-layouts: 15.1 us -> 2.55 us
  Pallas kernels: 93 us -> 102 us
    pallas_call x0 -> x1, Pallas kernels: none -> 9.47 us  [assemble(): pl.pallas_call(assemble_kernel, out_shape=jax.ShapeDtypeStruct((rows, par...]
    transpose x4 -> x0, local copies, waits for them, and re-layouts: 7.23 us -> none  [the longest x1 2.97 us: body(): factor[:, :, share:].transpose(1, 0, 2).reshape(-1, half_cols - eliminated)]
where the time goes in v4:
time: 452 us
  waiting for transfers between devices  271 us (60%)
  Pallas kernels  102 us (23%)
  blocking collectives  29.7 us (7%)
  other arithmetic  16.9 us (4%)
  between operations  13.5 us (3%)
  starting transfers between devices  9.83 us (2%)
  matrix products  5.68 us (1%)
    all_to_all x1, waiting for transfers between devices, body(): lax.all_to_all(send_block, ('col', 'front'), split_axis=0, concat_axis=0,...  99.5 us
    ppermute x1, waiting for transfers between devices, exchange_own(): lax.ppermute(leaving, 'col', [(i, (i + shift) % n_col) for i in range(n_c...  77.8 us
    pallas_call x1, Pallas kernels, cholesky_inverse(): pl.pallas_call(inverse_kernel, out_shape=(jax.ShapeDtypeStruct((n, n), jn...  62.3 us
    psum x1, waiting for transfers between devices, body(): square = lax.psum(square, ('col', 'row'))  61.7 us
    reduce_scatter x1, waiting for transfers between devices, body(): lax.psum_scatter(products, ('col', 'row'), scatter_dimension=0, tiled=True)  32 us
    pallas_call x1, Pallas kernels, gram(): pl.pallas_call(gram_kernel, out_shape=(jax.ShapeDtypeStruct((parts, elimi...  30.8 us
    all_to_all x1, blocking collectives, body(): lax.all_to_all(factor, ('col', 'row'), split_axis=0, concat_axis=0, tiled...  29.7 us
    pallas_call x1, Pallas kernels, assemble(): pl.pallas_call(assemble_kernel, out_shape=jax.ShapeDtypeStruct((rows, par...  9.47 us
  transfers between devices with their start and end apart: 4, of which 4 were waited for; matrix products, arithmetic and copies ran while one was open for 1% of the time, Pallas kernels for 14%

profile of v4, /device:TPU:0, one launch (start us, length us, event | category | flops | bytes accessed | tf_op | source)
XLA Modules:
  0.0 451.8 jit_solution(5868066937295135015)
XLA Ops:
  6.5 0.7 broadcast_multiply_fusion
  7.2 0.7 fusion.15
  7.9 1.2 reduce-window.6
  9.1 0.2 slice_reduce_fusion
  9.3 0.2 reduce-window.9
  9.5 0.1 add_bitcast_fusion
  9.6 0.7 fusion.14
  10.3 0.7 compare_select_fusion
  11.0 8.8 %scatter_custom_fusion = f32[1024,2048]{1,0:T(8,128)} fusion(s32[512]{0:T(512)S(1)} %bitcast.56, f32[512,2048]{1,0:T(8,128)} %param.5, f32[]{:T(128)} %constant.60.clone.1, s32[2048]{0:T(1024)S(1)} %iota_add_fusion, s32[512]{0:T(512)S(1)} %broadcast_multiply_fusion), kind=kCustom, calls=%fused_computation.1 | custom fusion | flops 2097152 | bytes 12594176 | tf_op jit(solution)/shard_map/scatter | solution.py:286
  19.8 0.0 copy-start
  19.8 7.6 %all-to-all-start = ((f32[8,128,2048]{2,1,0:T(8,128)}), f32[8,128,2048]{2,1,0:T(8,128)}, u32[]{:S(2)}, u32[]{:S(2)}) async-start(f32[8,128,2048]{2,1,0:T(8,128)} %bitcast.50), calls=%async_computation | async-start | bytes 16777216 | tf_op jit(solution)/shard_map/all_to_all | solution.py:288
  27.4 0.2 all-reduce.2.cloned.1.call-start
  27.7 0.0 copy-done
  27.7 1.3 dynamic-slice_bitcast_fusion
  28.9 1.8 collective-permute-start
  30.7 77.8 %collective-permute-done = f32[192,2048]{1,0:T(8,128)} collective-permute-done((f32[192,2048]{1,0:T(8,128)}, f32[192,2048]{1,0:T(8,128)}, u32[]{:S(2)}, u32[]{:S(2)}) %collective-permute-start) | collective-permute-done | bytes 1572896 | tf_op jit(solution)/shard_map/ppermute | solution.py:230
  108.5 1.6 fusion.9
  110.2 1.9 pad_maximum_fusion.own_lhs.refs_0_.refs_1_
  112.1 99.5 %all-to-all-done = f32[8,128,2048]{2,1,0:T(8,128)} async-done(((f32[8,128,2048]{2,1,0:T(8,128)}), f32[8,128,2048]{2,1,0:T(8,128)}, u32[]{:S(2)}, u32[]{:S(2)}) %all-to-all-start) | async-done | bytes 8388640 | tf_op jit(solution)/shard_map/all_to_all | solution.py:288
  211.6 30.8 %shard_map.46 = (f32[8,1024,384]{2,1,0:T(8,128)}, f32[10,256,256]{2,1,0:T(8,128)}) custom-call(f32[2,192,2048]{2,1,0:T(8,128)} %pad_maximum_fusion.own_lhs.refs_0_.refs_1_, f32[2,512,2048]{2,1,0:T(8,128)} %bitcast.11.child_lhs.refs_2_.refs_3_, f32[2,192,2048]{2,1,0:T(8,128)} %pad_maximum_fusion.own_lhs.refs_0_.refs_1_, ...), custom_call_target="tpu_custom_call" | custom-call | flops 17716740096 | bytes 28311552 | tf_op jit(solution)/shard_map/pallas_call | solution.py:89
  242.3 0.0 all-reduce.2.cloned.1.call-update
  242.4 0.3 reduce-scatter.2.cloned.1.call-start
  242.6 61.7 %all-reduce.2.cloned.1.call-done.blocks = f32[10,256,256]{2,1,0:T(8,128)} async-done(((f32[10,256,256]{2,1,0:T(8,128)}), f32[10,256,256]{2,1,0:T(8,128)}) %all-reduce.2.cloned.1.call-update) | async-done | bytes 2621456 | tf_op jit(solution)/shard_map/psum | solution.py:291
  304.4 0.0 reduce-scatter.2.cloned.1.call-update
  304.4 62.3 %shard_map.47 = (f32[1024,1024]{1,0:T(8,128)}, f32[1024,1024]{1,0:T(8,128)}) custom-call(f32[10,256,256]{2,1,0:T(8,128)} %all-reduce.2.cloned.1.call-done.blocks), custom_call_target="tpu_custom_call" | custom-call | flops 85899345920 | bytes 8388608 | tf_op jit(solution)/shard_map/pallas_call | solution.py:212
  366.7 1.1 constant_dynamic-slice_fusion
  367.8 32.0 %reduce-scatter.2.cloned.1.call-done = f32[1,1024,384]{2,1,0:T(8,128)} async-done(((f32[8,1024,384]{2,1,0:T(8,128)}), f32[1,1024,384]{2,1,0:T(8,128)}) %reduce-scatter.2.cloned.1.call-update) | async-done | bytes 1572880 | tf_op jit(solution)/shard_map/reduce_scatter | solution.py:293
  399.8 5.7 %fusion.7 = f32[1024,384]{1,0:T(8,128)S(1)} fusion(f32[1024,1024]{1,0:T(8,128)} %get-tuple-element.15, f32[1,1024,384]{2,1,0:T(8,128)} %reduce-scatter.2.cloned.1.call-done), kind=kOutput, calls=%fused_computation.10 | convolution fusion | flops 2415919104 | bytes 7340032 | tf_op jit(solution)/shard_map/dot_general | solution.py:295
  405.5 0.2 fusion.11
  405.6 0.1 pad_maximum_fusion.1
  405.8 29.7 %all_to_all.14.piece = f32[8,256,256]{2,1,0:T(8,128)} all-to-all(f32[8,256,256]{2,1,0:T(8,128)S(1)} %bitcast.51), channel_id=1, replica_groups=mesh['front'=4,'row'=4,'col'=2] {'col','row'}, dimensions={0} | all-to-all | bytes 4194304 | tf_op jit(solution)/shard_map/all_to_all | solution.py:305
  435.5 9.5 %shard_map.48 = f32[256,2048]{1,0:T(8,128)} custom-call(s32[1]{0:T(128)} %bitcast.col_ref, f32[8,256,256]{2,1,0:T(8,128)} %all_to_all.14.piece), custom_call_target="tpu_custom_call" | custom-call | tf_op jit(solution)/shard_map/pallas_call | solution.py:254
  (1 shorter events, 0.0 us)
Async XLA Ops:
  19.8 7.8 %copy-start = (f32[1,384,2048]{2,1,0:T(8,128)S(1)}, f32[1,384,2048]{2,1,0:T(8,128)}, u32[]{:S(2)}) copy-start(f32[1,384,2048]{2,1,0:T(8,128)} %param.4) | copy-start | bytes 9437188
  19.8 191.7 %all-to-all-start = ((f32[8,128,2048]{2,1,0:T(8,128)}), f32[8,128,2048]{2,1,0:T(8,128)}, u32[]{:S(2)}, u32[]{:S(2)}) async-start(f32[8,128,2048]{2,1,0:T(8,128)} %bitcast.50), calls=%async_computation | async-start | bytes 16777216 | tf_op jit(solution)/shard_map/all_to_all | solution.py:288
  27.4 277.0 %all-reduce.2.cloned.1.call-start = ((), (), s32[]{:S(2)}) async-start(), calls=%async_computation.3 | async-start | bytes 5242880 | tf_op jit(solution)/shard_map/psum | solution.py:291
  28.9 79.6 %collective-permute-start = (f32[192,2048]{1,0:T(8,128)}, f32[192,2048]{1,0:T(8,128)}, u32[]{:S(2)}, u32[]{:S(2)}) collective-permute-start(f32[192,2048]{1,0:T(8,128)} %dynamic-slice_bitcast_fusion), channel_id=1, source_target_pairs={{0,1},{1,0},{2,3},{3,2},{4,5},{5,4},{6,7},{7,6},{8,9},{9,8},{10,11... | collective-permute-start | bytes 4718600 | tf_op jit(solution)/shard_map/ppermute | solution.py:230
  242.4 157.4 %reduce-scatter.2.cloned.1.call-start = ((), (), s32[]{:S(2)}) async-start(), calls=%async_computation.4 | async-start | bytes 14155776 | tf_op jit(solution)/shard_map/reduce_scatter | solution.py:293
Sparse Core Ops, SparseCore 0:
  242.5 61.8 all-reduce.1
  307.9 91.8 reduce-scatter.1
